TPU v7x, 32 devices: a whole 2x2x4 slice. The times are simulated.
32 devices in a mesh: blk: 16 (over z, y, x), rhs: 2 (over core).
Axes of the slice: x: 2, y: 2, z: 4, core: 2. Of those that a mesh axis runs over, the one named last changes fastest.
Arguments:
- panel: int32 [1], replicated, may hold values from 0 to 19
- strips: bfloat16 [2, 6, 4096, 1024], P(None, None, 'blk'), may hold values from -0.078125 to 0.078125
- dinv_rows: bfloat16 [6, 4096, 1024], P(None, 'blk'), as said below
- fwd_state: float32 [6, 4096, 1024], P(None, 'blk', 'rhs'), may hold values from -6 to 6
- back_state: float32 [6, 4096, 1024], P(None, 'blk', 'rhs'), may hold values from -6 to 6
Outputs:
- fwd_out: float32 [6, 4096, 1024], P(None, 'blk', 'rhs')
- back_out: float32 [6, 4096, 1024], P(None, 'blk', 'rhs')
Inputs may be any that keep to these rules, and one draw needn't show every extreme that they name: `dinv_rows`: E_k transposed is lower triangular, with its diagonal between 0.5 and 1.5.
All inputs are finite; a program needn't handle non-finite values.
Results may differ from a plain program's by a relative error of at most 0.0015.
Values may be sent and summed in bfloat16 or wider, within the bound.
No kernel may reach another device: no remote copies, remote signals or barrier semaphores. Data moves between devices by JAX's collectives and lax.ppermute only.
A program may use at most 64 MiB of HBM per device.

v0:
```python
import jax
import jax.numpy as jnp
from jax import lax
from jax.sharding import PartitionSpec as P


def body(panel, strips, dinv_rows, fwd_state, back_state):
    tiles, span, columns = fwd_state.shape
    width = strips.shape[3]
    per_panel = width // span
    blocks = lax.axis_size("blk")
    device = lax.axis_index("blk")
    start = panel[0]
    slots = jnp.arange(tiles, dtype=jnp.int32)
    block_of = (slots * blocks + device) // per_panel

    def locate(k):
        offset = jnp.mod(device - per_panel * k, blocks)
        holds = offset < per_panel
        local = jnp.clip((per_panel * k + offset) // blocks, 0, tiles - 1)
        return (holds, local, jnp.minimum(offset, per_panel - 1))

    def forward(k, which, state):
        holds, local, offset = locate(k)
        strip = strips[which]
        current = lax.dynamic_index_in_dim(state, local, 0, keepdims=False).astype(jnp.bfloat16)
        inv_tile = lax.dynamic_index_in_dim(dinv_rows, local, 0, keepdims=False)
        partial_rows = lax.dot_general(
            inv_tile, current, (((0,), (0,)), ((), ())), preferred_element_type=jnp.float32
        )
        partial_rows = jnp.where(holds, partial_rows, 0.0)
        later = (block_of > k)[:, None, None]
        solved = lax.psum(partial_rows, "blk")
        delta = jnp.einsum(
            "atw,wc->atc", strip, solved.astype(jnp.bfloat16), preferred_element_type=jnp.float32
        )
        state = state - jnp.where(later, delta, 0.0)
        own_tile = lax.dynamic_slice_in_dim(solved, offset * span, span, 0)
        placed = lax.dynamic_update_index_in_dim(state, own_tile, local, 0)
        return jnp.where(holds, placed, state)

    def backward(k, which, state):
        holds, local, offset = locate(k)
        strip = strips[which]
        known = jnp.where((block_of > k)[:, None, None], state, 0.0).astype(jnp.bfloat16)
        term = -jnp.einsum("atw,atc->wc", strip, known, preferred_element_type=jnp.float32)
        current = lax.dynamic_index_in_dim(state, local, 0, keepdims=False)
        placed_rows = lax.dynamic_update_slice_in_dim(
            jnp.zeros((width, columns), jnp.float32), current, offset * span, 0
        )
        term = term + jnp.where(holds, placed_rows, 0.0)
        summed = lax.psum(term, "blk").astype(jnp.bfloat16)
        inv_tile = lax.dynamic_index_in_dim(dinv_rows, local, 0, keepdims=False)
        solved_tile = jnp.dot(inv_tile, summed, preferred_element_type=jnp.float32)
        placed = lax.dynamic_update_index_in_dim(state, solved_tile, local, 0)
        return jnp.where(holds, placed, state)

    fwd_out = forward(start, 0, fwd_state)
    fwd_out = forward(start + 1, 1, fwd_out)
    back_out = backward(start + 1, 1, back_state)
    back_out = backward(start, 0, back_out)
    return (fwd_out, back_out)


def solution(mesh):
    return jax.shard_map(
        body,
        mesh=mesh,
        in_specs=(
            P(),
            P(None, None, "blk", None),
            P(None, "blk", None),
            P(None, "blk", "rhs"),
            P(None, "blk", "rhs"),
        ),
        out_specs=(P(None, "blk", "rhs"), P(None, "blk", "rhs")),
        check_vma=False,
    )
```

profile of v0, /device:TPU:0, one launch (start us, length us, event | category | flops | bytes accessed | tf_op | source)
XLA Modules:
  0.0 337.4 jit_solution(13657352205158624932)
XLA Ops:
  7.2 0.0 all-reduce.5.cloned.1.call-start
  8.1 1.0 copy-done
  9.1 2.8 convolution_select_fusion.1
  11.9 0.0 all-reduce.7.cloned.1.call-start
  12.1 3.5 %copy.18 = f32[6,256,512]{1,2,0:T(8,128)} copy(f32[6,256,512]{2,1,0:T(8,128)} %param.8) | data formatting | bytes 6291456 | tf_op args[3]
  15.6 3.5 %copy.25 = f32[6,256,512]{1,2,0:T(8,128)} copy(f32[6,256,512]{2,1,0:T(8,128)} %param.9) | data formatting | bytes 6291456 | tf_op args[4]
  19.1 4.7 %bitcast_negate_fusion.1 = f32[512,1024]{1,0:T(8,128)S(1)} fusion(bf16[2,6,256,1024]{3,2,1,0:T(8,128)(2,1)} %param.6, f32[6,256,512]{1,2,0:T(8,128)} %copy.25, pred[6]{0:T(512)(128)(4,1)S(1)} %broadcast_compare_fusion), kind=kOutput, calls=%fused_computation.17 | convolution fusion | flops 1611923456 | bytes 8388614 | tf_op jit(solution)/shard_map/atw,atc->wc/dot_general | solution.py:46
  23.8 1.4 copy-done.1
  25.2 1.4 copy.39
  26.6 2.1 fusion.35
  28.7 113.7 %all-reduce.8 = bf16[1024,512]{0,1:T(8,128)(2,1)} all-reduce(f32[1024,512]{0,1:T(8,128)} %fusion.35), channel_id=1, replica_groups=mesh['blk'=16,'rhs'=2] {'blk'}, use_global_device_ids=true, to_apply=%region_2.3 | all-reduce | flops 524288 | bytes 3145728 | tf_op jit(solution)/shard_map/psum | solution.py:52
  142.4 2.6 fusion.25
  145.0 4.7 %bitcast_negate_fusion = f32[512,1024]{1,0:T(8,128)S(1)} fusion(bf16[2,6,256,1024]{3,2,1,0:T(8,128)(2,1)} %param.6, f32[6,256,512]{1,2,0:T(8,128)} %fusion.25, pred[6]{0:T(512)(128)(4,1)S(1)} %broadcast_compare_fusion.1), kind=kOutput, calls=%fused_computation.16 | convolution fusion | flops 1611923456 | bytes 8388614 | tf_op jit(solution)/shard_map/atw,atc->wc/dot_general | solution.py:46
  149.7 1.4 copy-done.2
  151.1 1.4 copy.42
  152.5 2.2 fusion.34
  154.6 2.6 all-reduce.5.cloned.1.call-done
  157.2 1.9 dynamic-slice_bitcast_fusion.1
  159.1 2.0 copy.19
  161.1 5.6 %bitcast_subtract_fusion.1 = f32[6,256,512]{1,2,0:T(8,128)S(1)} fusion(f32[6,256,512]{1,2,0:T(8,128)} %copy.18, pred[6]{0:T(512)(128)(4,1)S(1)} %broadcast_compare_fusion.1, bf16[2,6,256,1024]{3,2,1,0:T(8,128)(2,1)} %param.6, f32[1024,512]{1,0:T(8,128)} %all-reduce.5.cloned.1.call-done), kind=kOutput, calls=%fused_computation.5 | convolution fusion | flops 1612709888 | bytes 11534342 | tf_op jit(solution)/shard_map/atw,wc->atc/dot_general | solution.py:34
  166.7 0.1 select_dynamic-update-slice_fusion.1
  166.8 1.7 copy-done.5
  168.5 1.8 convolution_select_fusion
  170.3 112.5 %all-reduce.9 = bf16[1024,512]{0,1:T(8,128)(2,1)} all-reduce(f32[1024,512]{0,1:T(8,128)} %fusion.34), channel_id=1, replica_groups=mesh['blk'=16,'rhs'=2] {'blk'}, use_global_device_ids=true, to_apply=%region_3.4 | all-reduce | flops 524288 | bytes 3145728 | tf_op jit(solution)/shard_map/psum | solution.py:52
  282.8 2.6 fusion.27
  285.4 3.5 %copy.28 = f32[6,256,512]{2,1,0:T(8,128)} copy(f32[6,256,512]{1,2,0:T(8,128)} %fusion.27) | data formatting | bytes 6291456
  289.0 24.8 %all-reduce.7.cloned.1.call-done = f32[1024,512]{1,0:T(8,128)} async-done(((f32[1024,512]{1,0:T(8,128)}), f32[1024,512]{1,0:T(8,128)}) %all-reduce.7.cloned.1.call-update) | async-done | bytes 2097168 | tf_op jit(solution)/shard_map/psum | solution.py:33
  313.8 1.9 dynamic-slice_bitcast_fusion
  315.7 2.0 copy.21
  317.7 7.4 %bitcast_subtract_fusion = f32[6,256,512]{1,2,0:T(8,128)} fusion(f32[6,256,512]{1,2,0:T(8,128)} %copy-done.5, pred[6]{0:T(512)(128)(4,1)S(1)} %broadcast_compare_fusion, bf16[2,6,256,1024]{3,2,1,0:T(8,128)(2,1)} %param.6, f32[1024,512]{1,0:T(8,128)} %all-reduce.7.cloned.1.call-done), kind=kOutput, calls=%fused_computation | convolution fusion | flops 1612709888 | bytes 11534342 | tf_op jit(solution)/shard_map/atw,wc->atc/dot_general | solution.py:34
  325.1 1.9 select_dynamic-update-slice_fusion
  327.0 3.5 %copy.27 = f32[6,256,512]{2,1,0:T(8,128)} copy(f32[6,256,512]{1,2,0:T(8,128)} %select_dynamic-update-slice_fusion) | data formatting | bytes 6291456
  (12 shorter events, 0.1 us)
Async XLA Ops:
  7.2 1.9 copy-start
  7.2 150.0 %all-reduce.5.cloned.1.call-start = ((), (), s32[]{:S(2)}) async-start(), calls=%async_computation | async-start | bytes 4194304 | tf_op jit(solution)/shard_map/psum | solution.py:33
  11.9 301.9 %all-reduce.7.cloned.1.call-start = ((), (), s32[]{:S(2)}) async-start(), calls=%async_computation.1 | async-start | bytes 4194304 | tf_op jit(solution)/shard_map/psum | solution.py:33
  23.8 1.4 copy-start.1
  149.7 1.4 copy-start.2
  161.1 5.6 %copy-start.4 = (f32[1,256,512]{1,2,0:T(8,128)S(1)}, f32[1,256,512]{1,2,0:T(8,128)}, u32[]{:S(2)}) copy-start(f32[1,256,512]{1,2,0:T(8,128)} %copy.19) | copy-start | bytes 1572868
  166.8 1.7 copy-start.5
  317.7 7.4 %copy-start.3 = (f32[1,256,512]{1,2,0:T(8,128)S(1)}, f32[1,256,512]{1,2,0:T(8,128)}, u32[]{:S(2)}) copy-start(f32[1,256,512]{1,2,0:T(8,128)} %copy.21) | copy-start | bytes 1572868
Sparse Core Ops, SparseCore 0:
  14.1 143.0 all-reduce.4
  170.5 143.2 all-reduce.6
where the time goes:
time: 337 us
  blocking collectives  226 us (67%)
  matrix products  32.2 us (10%)
  local copies, waits for them, and re-layouts  30.1 us (9%)
  waiting for transfers between devices  27.5 us (8%)
  between operations  15 us (4%)
  other arithmetic  6.28 us (2%)
    psum x2, blocking collectives, backward(): summed = lax.psum(term, 'blk').astype(jnp.bfloat16)  226 us
    psum x2, waiting for transfers between devices, forward(): solved = lax.psum(partial_rows, 'blk')  27.4 us
    unnamed x18, local copies, waits for them, and re-layouts  22.3 us
    dot_general x2, matrix products, forward(): jnp.einsum('atw,wc->atc', strip, solved.astype(jnp.bfloat16), preferred_e...  12.9 us
    dot_general x2, matrix products, backward(): jnp.einsum('atw,atc->wc', strip, known, preferred_element_type=jnp.float32)  9.37 us
    broadcast_in_dim x4, local copies, waits for them, and re-layouts, forward(): placed = lax.dynamic_update_index_in_dim(state, own_tile, local, 0)  7.81 us
  transfers between devices with their start and end apart: 2, of which 2 were waited for; matrix products, arithmetic and copies ran while one was open for 10% of the time, Pallas kernels for 0%

commit v1 on v0

v1 whole, which is shorter than its diff:
```python
import jax
import jax.numpy as jnp
from jax import lax
from jax.experimental import pallas as pl
from jax.experimental.pallas import tpu as pltpu
from jax.sharding import PartitionSpec as P

BF = jnp.bfloat16
HF = jnp.float16
F32 = jnp.float32
SUM_SCALE = 4.0
VMEM = 100 * 1024 * 1024 // 2

NT = (((1,), (1,)), ((), ()))
NN = (((1,), (0,)), ((), ()))


def mm(a, b, dims):
    return lax.dot_general(a, b, dims, preferred_element_type=F32)


def plain_body(panel, strips, dinv_rows, fwd_state, back_state):
    tiles, span, columns = fwd_state.shape
    width = strips.shape[3]
    per_panel = width // span
    blocks = lax.axis_size("blk")
    device = lax.axis_index("blk")
    start = panel[0]
    slots = jnp.arange(tiles, dtype=jnp.int32)
    block_of = (slots * blocks + device) // per_panel

    def locate(k):
        offset = jnp.mod(device - per_panel * k, blocks)
        holds = offset < per_panel
        local = jnp.clip((per_panel * k + offset) // blocks, 0, tiles - 1)
        return (holds, local, jnp.minimum(offset, per_panel - 1))

    def forward(k, which, state):
        holds, local, offset = locate(k)
        strip = strips[which]
        current = lax.dynamic_index_in_dim(state, local, 0, keepdims=False).astype(BF)
        inv_tile = lax.dynamic_index_in_dim(dinv_rows, local, 0, keepdims=False)
        partial_rows = lax.dot_general(
            inv_tile, current, (((0,), (0,)), ((), ())), preferred_element_type=F32
        )
        partial_rows = jnp.where(holds, partial_rows, 0.0)
        later = (block_of > k)[:, None, None]
        solved = lax.psum(partial_rows, "blk")
        delta = jnp.einsum(
            "atw,wc->atc", strip, solved.astype(BF), preferred_element_type=F32
        )
        state = state - jnp.where(later, delta, 0.0)
        own_tile = lax.dynamic_slice_in_dim(solved, offset * span, span, 0)
        placed = lax.dynamic_update_index_in_dim(state, own_tile, local, 0)
        return jnp.where(holds, placed, state)

    def backward(k, which, state):
        holds, local, offset = locate(k)
        strip = strips[which]
        known = jnp.where((block_of > k)[:, None, None], state, 0.0).astype(BF)
        term = -jnp.einsum("atw,atc->wc", strip, known, preferred_element_type=F32)
        current = lax.dynamic_index_in_dim(state, local, 0, keepdims=False)
        placed_rows = lax.dynamic_update_slice_in_dim(
            jnp.zeros((width, columns), F32), current, offset * span, 0
        )
        term = term + jnp.where(holds, placed_rows, 0.0)
        summed = lax.psum(term, "blk").astype(BF)
        inv_tile = lax.dynamic_index_in_dim(dinv_rows, local, 0, keepdims=False)
        solved_tile = jnp.dot(inv_tile, summed, preferred_element_type=F32)
        placed = lax.dynamic_update_index_in_dim(state, solved_tile, local, 0)
        return jnp.where(holds, placed, state)

    fwd_out = forward(start, 0, fwd_state)
    fwd_out = forward(start + 1, 1, fwd_out)
    back_out = backward(start + 1, 1, back_state)
    back_out = backward(start, 0, back_out)
    return (fwd_out, back_out)


SLOT, OWNS, PANEL, PLANE, CHIP, CORE, KEEP, IS_A, FIRST, LOW = range(10)


def scalars(values):
    lane = lax.broadcasted_iota(jnp.int32, (16,), 0)
    out = jnp.zeros((16,), jnp.int32)
    for i, value in enumerate(values):
        out = jnp.where(lane == i, value.astype(jnp.int32), out)
    return out


def call(kernel, name, s, grid, ins, outs, shapes, arrays, scratch=(), aliases=None):
    return pl.pallas_call(
        kernel,
        grid_spec=pltpu.PrefetchScalarGridSpec(
            num_scalar_prefetch=1, grid=grid, in_specs=ins, out_specs=outs, scratch_shapes=list(scratch)
        ),
        out_shape=shapes,
        input_output_aliases=aliases or {},
        compiler_params=pltpu.CompilerParams(vmem_limit_bytes=VMEM),
        name=name,
    )(s, *arrays)


def whole(*shape):
    return pl.BlockSpec(shape, lambda i, s: (0,) * len(shape))


def shaped(dtype, *shape):
    return jax.ShapeDtypeStruct(shape, dtype)


def prep_kernel(s, e_ref, w_ref, f_ref, eh_ref, wh_ref, fq_ref):
    quarter = fq_ref.shape[2]
    eh_ref[...] = e_ref[0]
    wh_ref[...] = w_ref[0, 0]
    for q in range(4):
        fq_ref[q] = f_ref[0, :, q * quarter:(q + 1) * quarter]


def prep(s, strips, dinv_rows, fwd_state):
    tiles, span, columns = fwd_state.shape
    width = strips.shape[3]
    half, quarter = span // 2, columns // 4
    return call(
        prep_kernel, "prep", s, (1,),
        [
            pl.BlockSpec((1, half, width), lambda i, s: (s[SLOT], s[CORE], 0)),
            pl.BlockSpec((1, 1, half, width), lambda i, s: (0, s[SLOT], s[CORE], 0)),
            pl.BlockSpec((1, span, columns), lambda i, s: (s[SLOT], 0, 0)),
        ],
        [whole(half, width), whole(half, width), whole(4, span, quarter)],
        [shaped(BF, half, width), shaped(BF, half, width), shaped(F32, 4, span, quarter)],
        (dinv_rows, strips, fwd_state),
    )


def send_kernel(s, w_ref, b_ref, out_ref):
    a = pl.program_id(0)

    @pl.when(a == 0)
    def _():
        out_ref[...] = jnp.zeros_like(out_ref)

    @pl.when(4 * a + s[PLANE] > s[PANEL] + 1)
    def _():
        out_ref[...] += mm((b_ref[0] * SUM_SCALE).T.astype(BF), w_ref[0, 0], NN)


def keep_kernel(s, w_ref, b_ref, out_ref, copy_ref):
    a = pl.program_id(0)
    span = b_ref.shape[1]
    copy_ref[...] = b_ref[...]
    send_kernel(s, w_ref, b_ref, out_ref)

    @pl.when((a == s[SLOT]) & (s[OWNS] == 1))
    def _():
        at = pl.ds(pl.multiple_of(s[CHIP] * span, span), span)
        out_ref[:, at] = out_ref[:, at] - (b_ref[0] * SUM_SCALE).T


def sums_send(s, strips, back_state):
    tiles, span, columns = back_state.shape
    width = strips.shape[3]
    return call(
        send_kernel, "sums_send", s, (tiles,),
        [
            pl.BlockSpec((1, 1, span, width), lambda a, s: (1 - s[KEEP], jnp.maximum(a, s[FIRST]), 0, 0)),
            pl.BlockSpec((1, span, columns), lambda a, s: (jnp.maximum(a, s[FIRST]), 0, 0)),
        ],
        whole(columns, width),
        shaped(F32, columns, width),
        (strips, back_state),
    )


def sums_keep(s, strips, back_state):
    tiles, span, columns = back_state.shape
    width = strips.shape[3]
    tile = pl.BlockSpec((1, span, columns), lambda a, s: (a, 0, 0))
    return call(
        keep_kernel, "sums_keep", s, (tiles,),
        [
            pl.BlockSpec((1, 1, span, width), lambda a, s: (s[KEEP], jnp.maximum(a, s[FIRST]), 0, 0)),
            tile,
        ],
        [whole(columns, width), tile],
        [shaped(F32, columns, width), shaped(F32, *back_state.shape)],
        (strips, back_state),
    )


def join(full, d, mine, other, core):
    half = mine.shape[0]
    full[d, pl.ds(pl.multiple_of(core * half, half), half), :] = mine[...]
    full[d, pl.ds(pl.multiple_of((1 - core) * half, half), half), :] = other[...]


def split(x):
    high = x.astype(BF)
    return high, (x - high.astype(F32)).astype(BF)


def first_kernel(s, fq, own, m1, m2, m3, o1, o2, o3, hi, lo, e):
    span = fq.shape[1]
    e[0] = own[0]
    for d, mine, other in ((1, m1, o1), (2, m2, o2), (3, m3, o3)):
        join(e, d, mine, other, s[CORE])
    x = jnp.zeros(hi.shape, F32)
    for d in range(4):
        x += mm(fq[s[CHIP] ^ d].T.astype(BF), e[d], NN)
    high, low = split(x)
    hi[...] = high
    for q in range(4):
        lo[q] = low[:, q * span:(q + 1) * span]


def second_kernel(s, fq, xp, e, m0, m1, m2, m3, o0, o1, o2, o3, lo_a, hi, lo, w):
    span = fq.shape[1]
    for d, mine, other in ((0, m0, o0), (1, m1, o1), (2, m2, o2), (3, m3, o3)):
        join(w, d, mine, other, s[CORE])
    x = jnp.zeros(hi.shape, F32)
    for d in range(4):
        f = fq[s[CHIP] ^ d].T - mm(xp[...], w[d], NT)
        x += mm(f.astype(BF), e[d], NN)
    high, low = split(x)
    hi[...] = high

    @pl.when(s[IS_A] == 1)
    def _():
        lo[...] = lo_a[...]

    @pl.when(s[IS_A] == 0)
    def _():
        for q in range(4):
            lo[q] = low[:, q * span:(q + 1) * span]


def third_kernel(s, part, far, e, y, high):
    span = y.shape[2]
    rest = ((part[...] + far[...]) * (-1.0 / SUM_SCALE)).astype(BF)
    for d in range(4):
        q = s[CHIP] ^ d
        yq = mm(rest, e[d], NT)
        y[q] = yq
        high[:, pl.ds(pl.multiple_of(q * span, span), span)] = yq.astype(BF)


def fourth_kernel(s, part, far, high, e, w, y_b, y):
    span = y.shape[2]

    @pl.when(s[IS_A] == 0)
    def _():
        y[...] = y_b[...]

    @pl.when(s[IS_A] == 1)
    def _():
        rest = (part[...] + far[...]) * (-1.0 / SUM_SCALE)
        for d in range(4):
            at = pl.ds(pl.multiple_of((s[CHIP] ^ d) * span, span), span)
            rest -= mm(high[:, at], w[d], NN)
        rest = rest.astype(BF)
        for d in range(4):
            y[s[CHIP] ^ d] = mm(rest, e[d], NT)


def fill(x_full, pieces, chip):
    for d, piece in enumerate(pieces):
        x_full[chip ^ d] = piece[...]


def update_one_kernel(s, f_ref, w_ref, x0, x1, x2, x3, out_ref, x_full):
    a = pl.program_id(0)

    @pl.when(a == 0)
    def _():
        fill(x_full, (x0, x1, x2, x3), s[CHIP])

    later = 4 * a + s[PLANE] > s[PANEL] + 1

    @pl.when(later)
    def _():
        x = x_full[...].reshape(-1, x_full.shape[2])
        out_ref[0] = f_ref[0] - mm(w_ref[0, 0], x, NT)

    @pl.when(jnp.logical_not(later))
    def _():
        out_ref[...] = f_ref[...]


def update_two_kernel(s, f_ref, w_ref, x0, x1, x2, x3, p0, p1, p2, p3, lo_ref, out_ref, x_full):
    a = pl.program_id(0)
    span = f_ref.shape[1]
    quarter = lo_ref.shape[1]
    own = (a == s[SLOT]) & (s[OWNS] == 1)

    @pl.when(a == 0)
    def _():
        fill(x_full, (x0, x1, x2, x3), s[CHIP])

    @pl.when(4 * a + s[PLANE] > s[PANEL] + 1)
    def _():
        x = x_full[...].reshape(-1, x_full.shape[2])
        out_ref[0] = f_ref[0] - mm(w_ref[0, 0], x, NT)

    def solved(pieces):
        at = pl.ds(pl.multiple_of(s[CHIP] * span, span), span)
        for d, piece in enumerate(pieces):
            q = s[CHIP] ^ d
            x = piece[:, at].astype(F32) + lo_ref[q].astype(F32)
            out_ref[0, :, pl.ds(pl.multiple_of(q * quarter, quarter), quarter)] = x.T

    @pl.when(own & (s[IS_A] == 1))
    def _():
        solved((p0, p1, p2, p3))

    @pl.when(own & (s[IS_A] == 0))
    def _():
        solved((x0, x1, x2, x3))

    @pl.when((a == s[LOW]) & (4 * a + s[PLANE] <= s[PANEL] + 1) & jnp.logical_not(own))
    def _():
        out_ref[...] = f_ref[...]


def update_one(s, fwd_state, strips, pieces):
    tiles, span, columns = fwd_state.shape
    width = strips.shape[3]
    tile = pl.BlockSpec((1, span, columns), lambda a, s: (a, 0, 0))
    return call(
        update_one_kernel, "update_one", s, (tiles,),
        [tile, pl.BlockSpec((1, 1, span, width), lambda a, s: (0, jnp.maximum(a, s[FIRST]), 0, 0))]
        + [whole(columns // 4, width)] * 4,
        tile, shaped(F32, *fwd_state.shape),
        (fwd_state, strips, *pieces),
        scratch=[pltpu.VMEM((4, columns // 4, width), BF)],
    )


def update_two(s, state, strips, pieces, pieces_p, lo):
    tiles, span, columns = state.shape
    width = strips.shape[3]
    tile = pl.BlockSpec((1, span, columns), lambda a, s: (jnp.maximum(a, s[LOW]), 0, 0))
    return call(
        update_two_kernel, "update_two", s, (tiles,),
        [tile, pl.BlockSpec((1, 1, span, width), lambda a, s: (1, jnp.maximum(a, s[FIRST]), 0, 0))]
        + [whole(columns // 4, width)] * 8 + [whole(*lo.shape)],
        tile, shaped(F32, *state.shape),
        (state, strips, *pieces, *pieces_p, lo),
        scratch=[pltpu.VMEM((4, columns // 4, width), BF)],
        aliases={1: 0},
    )


def place_kernel(s, copy_ref, y_ref, out_ref):
    quarter = y_ref.shape[1]

    @pl.when(s[OWNS] == 1)
    def _():
        for q in range(4):
            out_ref[0, :, q * quarter:(q + 1) * quarter] = y_ref[q].T

    @pl.when(s[OWNS] == 0)
    def _():
        out_ref[...] = copy_ref[...]


def place(s, copy, y):
    tiles, span, columns = copy.shape
    tile = pl.BlockSpec((1, span, columns), lambda i, s: (s[SLOT], 0, 0))
    return call(
        place_kernel, "place", s, (1,), [tile, whole(*y.shape)], tile,
        shaped(F32, *copy.shape), (copy, y), aliases={1: 0},
    )


def after(x, *waits):
    return lax.optimization_barrier((x,) + waits)[0]


def plane_body(panel, strips, dinv_rows, fwd_state, back_state):
    tiles, span, columns = fwd_state.shape
    width = strips.shape[3]
    half, quarter = span // 2, columns // 4
    device = lax.axis_index("blk")
    plane, chip, core = device // 4, device % 4, lax.axis_index("rhs")
    start = panel[0]
    home = lax.rem(start, 4)
    is_a = plane == home
    is_b = plane == lax.rem(start + 1, 4)
    groups = [[4 * z + j for j in range(4)] for z in range(4)]

    def exchange(x):
        return lax.all_to_all(x, "blk", 0, 0, axis_index_groups=groups, tiled=True)

    def permute(x, to):
        return lax.ppermute(x, "blk", [(i, to(i)) for i in range(16)])

    def up(x):
        return permute(x, lambda i: (i + 4) % 16)

    def down(x):
        return permute(x, lambda i: (i + 12) % 16)

    def across(x):
        return permute(x, lambda i: i ^ 8)

    def gather(x):
        return [permute(x, lambda i, d=d: i ^ d) for d in (1, 2, 3)]

    def swap(x):
        return lax.ppermute(x, "rhs", [(0, 1), (1, 0)])

    slot = start // 4 + jnp.where(is_b & (home == 3), 1, 0)
    keep = lax.rem(plane + start + 1, 2) == 0
    first_later = jnp.clip((start + 5 - plane) // 4, 0, tiles - 1)
    low = jnp.minimum(first_later, jnp.where(is_a | is_b, slot, tiles - 1))
    s = scalars([slot, is_a | is_b, start, plane, chip, core, keep, is_a, first_later, low])

    sent = sums_send(s, strips, back_state).astype(HF)
    got = permute(sent, lambda i: i ^ 4)

    eh, wh, fq = prep(s, strips, dinv_rows, fwd_state)
    e_mine = gather(eh)
    fq = exchange(fq.reshape(4 * span, quarter)).reshape(4, span, quarter)
    wh = jnp.where(is_a, down(wh), wh)
    e_other = [swap(x) for x in e_mine]

    piece = shaped(BF, quarter, width)
    lows = shaped(BF, 4, quarter, span)
    matrix = shaped(BF, 4, span, width)
    thin, thick = whole(half, width), whole(quarter, width)

    hi_p, lo_p, e = call(
        first_kernel, "first", s, (1,),
        [whole(4, span, quarter), pl.BlockSpec((1, span, width), lambda i, s: (s[SLOT], 0, 0))] + [thin] * 6,
        [thick, whole(4, quarter, span), whole(4, span, width)], [piece, lows, matrix],
        (fq, dinv_rows, *e_mine, *e_other),
    )
    below = up(hi_p)
    w_mine = [wh] + gather(wh)
    w_other = [swap(x) for x in w_mine]
    kept, copy = sums_keep(s, strips, back_state)

    xp = jnp.where(is_a, hi_p, below)
    xp_far = across(xp)
    hi_q, lo, w = call(
        second_kernel, "second", s, (1,),
        [whole(4, span, quarter), thick, whole(4, span, width)] + [thin] * 8 + [whole(4, quarter, span)],
        [thick, whole(4, quarter, span), whole(4, span, width)], [piece, lows, matrix],
        (fq, xp, e, *w_mine, *w_other, lo_p),
    )

    def spread(first):
        source = (first + 1) % 4

        def run(x):
            total = x
            for z in range(4):
                if z != source:
                    total = total + lax.ppermute(
                        x, "blk", [(4 * source + j, 4 * z + j) for j in range(4)]
                    )
            return total

        return run

    hi_q = jnp.where(is_b, hi_q, jnp.zeros_like(hi_q))
    xq = lax.switch(home, [spread(z) for z in range(4)], hi_q)
    lo_own = exchange(lo.reshape(columns, span)).reshape(4, quarter, span)
    xp = jnp.where(is_a | is_b, xp, xp_far)
    xp_all = [xp] + gather(xp)
    state = update_one(s, fwd_state, strips, xp_all)
    xq_all = [xq] + gather(xq)
    fwd_out = update_two(s, state, strips, xq_all, xp_all, lo_own)

    pair = (kept + got.astype(F32)).astype(HF)
    parts = exchange(pair).reshape(4, quarter, width)
    part = jnp.sum(parts.astype(F32), axis=0)
    far = across(part.astype(HF)).astype(F32)
    y_b, high = call(
        third_kernel, "third", s, (1,), [thick, thick, whole(4, span, width)],
        [whole(4, quarter, span), thick], [shaped(F32, 4, quarter, span), piece],
        (part, far, e),
    )
    high = down(high)
    y = call(
        fourth_kernel, "fourth", s, (1,),
        [thick, thick, thick, whole(4, span, width), whole(4, span, width), whole(4, quarter, span)],
        whole(4, quarter, span), shaped(F32, 4, quarter, span),
        (part, far, high, e, w, y_b),
    )
    y_own = exchange(y.reshape(columns, span)).reshape(4, quarter, span)
    back_out = place(s, copy, y_own)
    return fwd_out, back_out


def body(panel, strips, dinv_rows, fwd_state, back_state):
    tiles, span, columns = fwd_state.shape
    width = strips.shape[3]
    blocks = lax.axis_size("blk")
    regular = (
        blocks == 16
        and lax.axis_size("rhs") == 2
        and width == 4 * span
        and span % 256 == 0
        and columns % 512 == 0
    )
    chosen = plane_body if regular else plain_body
    return chosen(panel, strips, dinv_rows, fwd_state, back_state)


def solution(mesh):
    return jax.shard_map(
        body,
        mesh=mesh,
        in_specs=(
            P(),
            P(None, None, "blk", None),
            P(None, "blk", None),
            P(None, "blk", "rhs"),
            P(None, "blk", "rhs"),
        ),
        out_specs=(P(None, "blk", "rhs"), P(None, "blk", "rhs")),
        check_vma=False,
    )
```

time: 337 us -> 182 us (0.54)
  blocking collectives: 226 us -> 0 us
  starting transfers between devices: 0.08 us -> 59.9 us
  Pallas kernels: 0 us -> 44 us
  matrix products: 32.2 us -> 0 us
  waiting for transfers between devices: 27.5 us -> 57.7 us
  local copies, waits for them, and re-layouts: 30.1 us -> 11.9 us
  between operations: 15 us -> 1.6 us
    psum x2 -> x0, blocking collectives: 226 us -> none  [backward(): summed = lax.psum(term, 'blk').astype(jnp.bfloat16)]
    ppermute x0 -> x28, waiting for transfers between devices: none -> 57.6 us  [the longest x18 48.4 us: permute(): return lax.ppermute(x, 'blk', [(i, to(i)) for i in range(16)])]
    pallas_call x0 -> x10, Pallas kernels: none -> 44 us  [call(): pl.pallas_call(kernel, grid_spec=pltpu.PrefetchScalarGridSpec(num_scalar_...]
    ppermute x0 -> x28, starting transfers between devices: none -> 44 us  [the longest x18 33.7 us: permute(): return lax.ppermute(x, 'blk', [(i, to(i)) for i in range(16)])]
    dot_general x8 -> x0, matrix products: 32.2 us -> none  [the longest x2 12.9 us: forward(): jnp.einsum('atw,wc->atc', strip, solved.astype(jnp.bfloat16), preferred_e...]
    psum x2 -> x0, waiting for transfers between devices: 27.4 us -> none  [forward(): solved = lax.psum(partial_rows, 'blk')]
    all_to_all x0 -> x4, starting transfers between devices: none -> 15.9 us  [exchange(): return lax.all_to_all(x, 'blk', 0, 0, axis_index_groups=groups, tiled=True)]
    unnamed x18 -> x44, local copies, waits for them, and re-layouts: 22.3 us -> 11.9 us
  transfers between devices with their start and end apart: 2 -> 32, of which waited for: 2 -> 8; matrix products, arithmetic and copies ran while one was open for 10% -> 4% of each run, Pallas kernels for 0% -> 20%
where the time goes in v1:
time: 182 us
  starting transfers between devices  59.9 us (33%)
  waiting for transfers between devices  57.7 us (32%)
  Pallas kernels  44 us (24%)
  local copies, waits for them, and re-layouts  11.9 us (7%)
  other arithmetic  7.27 us (4%)
    ppermute x18, waiting for transfers between devices, permute(): return lax.ppermute(x, 'blk', [(i, to(i)) for i in range(16)])  48.4 us
    pallas_call x10, Pallas kernels, call(): pl.pallas_call(kernel, grid_spec=pltpu.PrefetchScalarGridSpec(num_scalar_...  44 us
    ppermute x18, starting transfers between devices, permute(): return lax.ppermute(x, 'blk', [(i, to(i)) for i in range(16)])  33.7 us
    all_to_all x4, starting transfers between devices, exchange(): return lax.all_to_all(x, 'blk', 0, 0, axis_index_groups=groups, tiled=True)  15.9 us
    unnamed x44, local copies, waits for them, and re-layouts  11.9 us
    ppermute x3, starting transfers between devices, run(): lax.ppermute(x, 'blk', [(4 * source + j, 4 * z + j) for j in range(4)])  9.24 us
    ppermute x3, waiting for transfers between devices, run(): lax.ppermute(x, 'blk', [(4 * source + j, 4 * z + j) for j in range(4)])  9.2 us
  transfers between devices with their start and end apart: 32, of which 8 were waited for; matrix products, arithmetic and copies ran while one was open for 4% of the time, Pallas kernels for 20%

profile of v1, /device:TPU:0, one launch (start us, length us, event | category | flops | bytes accessed | tf_op | source)
XLA Modules:
  0.0 182.4 jit_solution(15693380159258210913)
XLA Ops:
  1.4 4.3 %sums_send.1 = f32[512,1024]{1,0:T(8,128)S(1)} custom-call(s32[16]{0:T(128)S(1)} %compare_select_fusion.9.s, bf16[2,6,256,1024]{3,2,1,0:T(8,128)(2,1)} %w_ref.9, f32[6,256,512]{2,1,0:T(8,128)} %b_ref.3), custom_call_target="tpu_custom_call" | custom-call | tf_op jit(solution)/shard_map/sums_send/pallas_call | solution.py:92
  5.9 4.2 %collective-permute-start.34 = (f16[512,1024]{1,0:T(8,128)(2,1)S(1)}, f16[512,1024]{1,0:T(8,128)(2,1)}, u32[]{:S(2)}, u32[]{:S(2)}) collective-permute-start(f16[512,1024]{1,0:T(8,128)(2,1)S(1)} %convert_element_type.30), channel_id=1, source_target_pairs={{0,8},{2,10},{4,12},{6,14},{8,0},{10,2},{12,4},{14,6},{16,24},{18,... | collective-permute-start | bytes 3145736 | tf_op jit(solution)/shard_map/ppermute | solution.py:396
  10.1 2.6 %prep.1 = (bf16[128,1024]{1,0:T(8,128)(2,1)S(1)}, bf16[128,1024]{1,0:T(8,128)(2,1)S(1)}, f32[4,256,128]{2,1,0:T(8,128)}) custom-call(s32[16]{0:T(128)S(1)} %compare_select_fusion.9.s, bf16[6,256,1024]{2,1,0:T(8,128)(2,1)} %own.1, bf16[2,6,256,1024]{3,2,1,0:T(8,128)(2,1)} %w_ref.9, f32[6,256,512]{2,1,0:T(8,128)} %f_ref.3), custom_call_target="tpu_custom_call" | custom-call | tf_op jit(solution)/shard_map/prep/pallas_call | solution.py:92
  12.6 3.7 %all-to-all-start = ((f32[4,256,128]{2,1,0:T(8,128)}), f32[4,256,128]{2,1,0:T(8,128)S(1)}, u32[]{:S(2)}, u32[]{:S(2)}) async-start(f32[4,256,128]{2,1,0:T(8,128)} %get-tuple-element.24), calls=%async_computation | async-start | bytes 1048576 | tf_op jit(solution)/shard_map/all_to_all | solution.py:393
  16.4 2.0 %collective-permute-start.12 = (bf16[128,1024]{1,0:T(8,128)(2,1)S(1)}, bf16[128,1024]{1,0:T(8,128)(2,1)S(1)}, u32[]{:S(2)}, u32[]{:S(2)}) collective-permute-start(bf16[128,1024]{1,0:T(8,128)(2,1)S(1)} %get-tuple-element.25), channel_id=1, source_target_pairs={{0,2},{2,0},{4,6},{6,4},{8,10},{10,8},{12,14},{14,12},{16,18},{18,... | collective-permute-start | bytes 786440 | tf_op jit(solution)/shard_map/ppermute | solution.py:396
  18.4 7.1 %sums_keep.1 = (f32[512,1024]{1,0:T(8,128)S(1)}, f32[6,256,512]{2,1,0:T(8,128)}) custom-call(s32[16]{0:T(128)S(1)} %compare_select_fusion.9.s, bf16[2,6,256,1024]{3,2,1,0:T(8,128)(2,1)} %w_ref.9, f32[6,256,512]{2,1,0:T(8,128)} %b_ref.3), custom_call_target="tpu_custom_call" | custom-call | tf_op jit(solution)/shard_map/sums_keep/pallas_call | solution.py:92
  25.5 7.8 %collective-permute-done.34 = f16[512,1024]{1,0:T(8,128)(2,1)} collective-permute-done((f16[512,1024]{1,0:T(8,128)(2,1)S(1)}, f16[512,1024]{1,0:T(8,128)(2,1)}, u32[]{:S(2)}, u32[]{:S(2)}) %collective-permute-start.34) | collective-permute-done | bytes 1048608 | tf_op jit(solution)/shard_map/ppermute | solution.py:396
  33.3 2.7 %add_convert_fusion = f16[512,1024]{1,0:T(8,128)(2,1)} fusion(f32[512,1024]{1,0:T(8,128)S(1)} %get-tuple-element.33, f16[512,1024]{1,0:T(8,128)(2,1)} %collective-permute-done.34), kind=kLoop, calls=%fused_computation.5 | loop fusion | flops 1572864 | bytes 4194304 | tf_op jit(solution)/shard_map/convert_element_type | solution.py:476
  36.0 4.2 %all-to-all-start.2 = ((f16[4,128,1024]{2,1,0:T(8,128)(2,1)}), f16[4,128,1024]{2,1,0:T(8,128)(2,1)}, u32[]{:S(2)}, u32[]{:S(2)}) async-start(f16[4,128,1024]{2,1,0:T(8,128)(2,1)} %bitcast.1), calls=%async_computation.2 | async-start | bytes 2097152 | tf_op jit(solution)/shard_map/all_to_all | solution.py:393
  43.7 3.8 %collective-permute-start.23 = (bf16[128,1024]{1,0:T(8,128)(2,1)S(1)}, bf16[128,1024]{1,0:T(8,128)(2,1)S(1)}, u32[]{:S(2)}, u32[]{:S(2)}) collective-permute-start(bf16[128,1024]{1,0:T(8,128)(2,1)S(1)} %get-tuple-element.28), channel_id=1, source_target_pairs={{0,24},{2,26},{4,28},{6,30},{8,0},{10,2},{12,4},{14,6},{16,8},{18,... | collective-permute-start | bytes 786440 | tf_op jit(solution)/shard_map/ppermute | solution.py:396
  47.5 17.3 %collective-permute-done.13.m2 = bf16[128,1024]{1,0:T(8,128)(2,1)S(1)} collective-permute-done((bf16[128,1024]{1,0:T(8,128)(2,1)S(1)}, bf16[128,1024]{1,0:T(8,128)(2,1)S(1)}, u32[]{:S(2)}, u32[]{:S(2)}) %collective-permute-start.13) | collective-permute-done | bytes 262176 | tf_op jit(solution)/shard_map/ppermute | solution.py:396
  68.9 3.0 %first.1 = (bf16[128,1024]{1,0:T(8,128)(2,1)S(1)}, bf16[4,128,256]{2,1,0:T(8,128)(2,1)S(1)}, bf16[4,256,1024]{2,1,0:T(8,128)(2,1)}) custom-call(s32[16]{0:T(128)S(1)} %compare_select_fusion.9.s, f32[4,256,128]{2,1,0:T(8,128)S(1)} %all-to-all-done.fq, bf16[6,256,1024]{2,1,0:T(8,128)(2,1)} %own.1, bf16[128,1024]{1,0:T(8,128)(2,1)S(1)} %collective-permute-done.12.m1, ...), custom_call_target="tpu_custom_call" | custom-call | tf_op jit(solution)/shard_map/first/pallas_call | solution.py:92
  74.6 5.8 %collective-permute-done.25.m2 = bf16[128,1024]{1,0:T(8,128)(2,1)S(1)} collective-permute-done((bf16[128,1024]{1,0:T(8,128)(2,1)S(1)}, bf16[128,1024]{1,0:T(8,128)(2,1)S(1)}, u32[]{:S(2)}, u32[]{:S(2)}) %collective-permute-start.25) | collective-permute-done | bytes 262176 | tf_op jit(solution)/shard_map/ppermute | solution.py:396
  83.3 2.4 %collective-permute-start.35 = (f16[128,1024]{1,0:T(8,128)(2,1)}, f16[128,1024]{1,0:T(8,128)(2,1)}, u32[]{:S(2)}, u32[]{:S(2)}) collective-permute-start(f16[128,1024]{1,0:T(8,128)(2,1)} %convert_element_type.34), channel_id=1, source_target_pairs={{0,16},{2,18},{4,20},{6,22},{8,24},{10,26},{12,28},{14,30},{16,0},... | collective-permute-start | bytes 786440 | tf_op jit(solution)/shard_map/ppermute | solution.py:396
  96.0 5.4 %second.1 = (bf16[128,1024]{1,0:T(8,128)(2,1)S(1)}, bf16[4,128,256]{2,1,0:T(8,128)(2,1)S(1)}, bf16[4,256,1024]{2,1,0:T(8,128)(2,1)}) custom-call(s32[16]{0:T(128)S(1)} %compare_select_fusion.9.s, f32[4,256,128]{2,1,0:T(8,128)S(1)} %all-to-all-done.fq, bf16[128,1024]{1,0:T(8,128)(2,1)S(1)} %broadcast_select_fusion.2.xp, ...), custom_call_target="tpu_custom_call" | custom-call | tf_op jit(solution)/shard_map/second/pallas_call | solution.py:92
  102.8 4.1 %all-to-all-start.1 = ((bf16[4,128,256]{2,1,0:T(8,128)(2,1)}), bf16[4,128,256]{2,1,0:T(8,128)(2,1)}, u32[]{:S(2)}, u32[]{:S(2)}) async-start(bf16[4,128,256]{2,1,0:T(8,128)(2,1)} %copy-done.7), calls=%async_computation.1 | async-start | bytes 524288 | tf_op jit(solution)/shard_map/all_to_all | solution.py:393
  107.8 2.1 %third.1 = (f32[4,128,256]{2,1,0:T(8,128)S(1)}, bf16[128,1024]{1,0:T(8,128)(2,1)}) custom-call(s32[16]{0:T(128)S(1)} %compare_select_fusion.9.s, f32[128,1024]{1,0:T(8,128)S(1)} %convert_reduce_fusion.part, f32[128,1024]{1,0:T(8,128)S(1)} %convert_element_type.35.far, bf16[4,256,1024]{2,1,0:T(8,128)(2,1)S(1)} %copy-done), custom_call_target="tpu_custom_call" | custom-call | tf_op jit(solution)/shard_map/third/pallas_call | solution.py:92
  109.9 3.4 %collective-permute-start.36 = (bf16[128,1024]{1,0:T(8,128)(2,1)}, bf16[128,1024]{1,0:T(8,128)(2,1)S(1)}, u32[]{:S(2)}, u32[]{:S(2)}) collective-permute-start(bf16[128,1024]{1,0:T(8,128)(2,1)} %get-tuple-element.34), channel_id=1, source_target_pairs={{0,24},{2,26},{4,28},{6,30},{8,0},{10,2},{12,4},{14,6},{16,8},{18,... | collective-permute-start | bytes 786440 | tf_op jit(solution)/shard_map/ppermute | solution.py:396
  113.4 2.0 %collective-permute-start.20 = (bf16[128,1024]{1,0:T(8,128)(2,1)S(1)}, bf16[128,1024]{1,0:T(8,128)(2,1)S(1)}, u32[]{:S(2)}, u32[]{:S(2)}) collective-permute-start(bf16[128,1024]{1,0:T(8,128)(2,1)S(1)} %broadcast_select_fusion.3.x0.p0), channel_id=1, source_target_pairs={{0,2},{2,0},{4,6},{6,4},{8,10},{10,8},{12,14},{14,12},{16,18},{18,... | collective-permute-start | bytes 786440 | tf_op jit(solution)/shard_map/ppermute | solution.py:396
  115.5 3.5 %collective-permute-done.36.high = bf16[128,1024]{1,0:T(8,128)(2,1)S(1)} collective-permute-done((bf16[128,1024]{1,0:T(8,128)(2,1)}, bf16[128,1024]{1,0:T(8,128)(2,1)S(1)}, u32[]{:S(2)}, u32[]{:S(2)}) %collective-permute-start.36) | collective-permute-done | bytes 262176 | tf_op jit(solution)/shard_map/ppermute | solution.py:396
  120.0 3.6 %fourth.1 = f32[4,128,256]{2,1,0:T(8,128)} custom-call(s32[16]{0:T(128)S(1)} %compare_select_fusion.9.s, f32[128,1024]{1,0:T(8,128)S(1)} %convert_reduce_fusion.part, f32[128,1024]{1,0:T(8,128)S(1)} %convert_element_type.35.far, bf16[128,1024]{1,0:T(8,128)(2,1)S(1)} %collective-permute-done.36.high, bf16[4,256,1024]{2,1,0:T(8,128)(2,1)} %get-tuple-element.27.e, ...), custom_call_target="tpu_custom_call" | custom-call | tf_op jit(solution)/shard_map/fourth/pallas_call | solution.py:92
  123.6 3.9 %all-to-all-start.3 = ((f32[4,128,256]{2,1,0:T(8,128)}), f32[4,128,256]{2,1,0:T(8,128)S(1)}, u32[]{:S(2)}, u32[]{:S(2)}) async-start(f32[4,128,256]{2,1,0:T(8,128)} %fourth.1), calls=%async_computation.3 | async-start | bytes 1048576 | tf_op jit(solution)/shard_map/all_to_all | solution.py:393
  127.5 18.6 %conditional.1 = (bf16[128,1024]{1,0:T(8,128)(2,1)S(1)}) conditional(s32[]{:T(128)} %clamp.3, bf16[128,1024]{1,0:T(8,128)(2,1)S(1)} %broadcast_select_fusion, bf16[128,1024]{1,0:T(8,128)(2,1)S(1)} %broadcast_select_fusion, bf16[128,1024]{1,0:T(8,128)(2,1)S(1)} %broadcast_select_fusion, ...), branch_computations={%region_0.1_spmd, %region_1.2_spmd, %region_2.3_spmd, %region_3.4_... | conditional | flops 393216 | bytes 4456576 | solution.py:468
  127.5 3.3 %collective-permute-start.10 = (bf16[128,1024]{1,0:T(8,128)(2,1)S(1)}, bf16[128,1024]{1,0:T(8,128)(2,1)S(1)}, u32[]{:S(2)}, u32[]{:S(2)}) collective-permute-start(bf16[128,1024]{1,0:T(8,128)(2,1)S(1)} %param.3), channel_id=1, source_target_pairs={{0,16},{2,18},{4,20},{6,22},{1,17},{3,19},{5,21},{7,23}} | collective-permute-start | bytes 786440 | tf_op jit(solution)/shard_map/cond/branch_3_fun/ppermute | solution.py:460
  130.8 4.7 %collective-permute-start.11 = (bf16[128,1024]{1,0:T(8,128)(2,1)S(1)}, bf16[128,1024]{1,0:T(8,128)(2,1)S(1)}, u32[]{:S(2)}, u32[]{:S(2)}) collective-permute-start(bf16[128,1024]{1,0:T(8,128)(2,1)S(1)} %param.3), channel_id=1, source_target_pairs={{0,24},{2,26},{4,28},{6,30},{1,25},{3,27},{5,29},{7,31}} | collective-permute-start | bytes 786440 | tf_op jit(solution)/shard_map/cond/branch_3_fun/ppermute | solution.py:460
  136.8 5.4 %collective-permute-done.11 = bf16[128,1024]{1,0:T(8,128)(2,1)S(1)} collective-permute-done((bf16[128,1024]{1,0:T(8,128)(2,1)S(1)}, bf16[128,1024]{1,0:T(8,128)(2,1)S(1)}, u32[]{:S(2)}, u32[]{:S(2)}) %collective-permute-start.11) | collective-permute-done | bytes 262176 | tf_op jit(solution)/shard_map/cond/branch_3_fun/ppermute | solution.py:460
  142.2 3.8 %collective-permute-done.9 = bf16[128,1024]{1,0:T(8,128)(2,1)S(1)} collective-permute-done((bf16[128,1024]{1,0:T(8,128)(2,1)S(1)}, bf16[128,1024]{1,0:T(8,128)(2,1)S(1)}, u32[]{:S(2)}, u32[]{:S(2)}) %collective-permute-start.9) | collective-permute-done | bytes 262176 | tf_op jit(solution)/shard_map/cond/branch_3_fun/ppermute | solution.py:460
  146.1 2.0 %collective-permute-start.21 = (bf16[128,1024]{1,0:T(8,128)(2,1)S(1)}, bf16[128,1024]{1,0:T(8,128)(2,1)S(1)}, u32[]{:S(2)}, u32[]{:S(2)}) collective-permute-start(bf16[128,1024]{1,0:T(8,128)(2,1)S(1)} %broadcast_select_fusion.3.x0.p0), channel_id=1, source_target_pairs={{0,4},{2,6},{4,0},{6,2},{8,12},{10,14},{12,8},{14,10},{16,20},{18,... | collective-permute-start | bytes 786440 | tf_op jit(solution)/shard_map/ppermute | solution.py:396
  153.0 13.5 %collective-permute-done.21.x2.p2 = bf16[128,1024]{1,0:T(8,128)(2,1)S(1)} collective-permute-done((bf16[128,1024]{1,0:T(8,128)(2,1)S(1)}, bf16[128,1024]{1,0:T(8,128)(2,1)S(1)}, u32[]{:S(2)}, u32[]{:S(2)}) %collective-permute-start.21) | collective-permute-done | bytes 262176 | tf_op jit(solution)/shard_map/ppermute | solution.py:396
  166.5 7.0 %update_one.1.f_ref = f32[6,256,512]{2,1,0:T(8,128)} custom-call(s32[16]{0:T(128)S(1)} %compare_select_fusion.9.s, f32[6,256,512]{2,1,0:T(8,128)} %f_ref.3, bf16[2,6,256,1024]{3,2,1,0:T(8,128)(2,1)} %w_ref.9, bf16[128,1024]{1,0:T(8,128)(2,1)S(1)} %broadcast_select_fusion.3.x0.p0, bf16[128,1024]{1,0:T(8,128)(2,1)S(1)} %collective-permute-done.20.x1.p1, ...), custom_call_target="tpu_custom_call" | custom-call | tf_op jit(solution)/shard_map/update_one/pallas_call | solution.py:92
  173.5 6.3 %update_two.1 = f32[6,256,512]{2,1,0:T(8,128)} custom-call(s32[16]{0:T(128)S(1)} %compare_select_fusion.9.s, f32[6,256,512]{2,1,0:T(8,128)} %update_one.1.f_ref, bf16[2,6,256,1024]{3,2,1,0:T(8,128)(2,1)} %w_ref.9, bf16[128,1024]{1,0:T(8,128)(2,1)S(1)} %get-tuple-element.37.x0, ...), custom_call_target="tpu_custom_call", output_to_operand_aliasing={{}: (1, {})} | custom-call | tf_op jit(solution)/shard_map/update_two/pallas_call | solution.py:92
  179.8 2.6 %place.1 = f32[6,256,512]{2,1,0:T(8,128)} custom-call(s32[16]{0:T(128)S(1)} %compare_select_fusion.9.s, f32[6,256,512]{2,1,0:T(8,128)} %get-tuple-element.32.copy_ref, f32[4,128,256]{2,1,0:T(8,128)S(1)} %all-to-all-done.3.y_ref), custom_call_target="tpu_custom_call", output_to_operand_aliasing={{}: (1, {})} | custom-call | tf_op jit(solution)/shard_map/place/pallas_call | solution.py:92
  (98 shorter events, 33.3 us)
Async XLA Ops:
  5.9 27.4 %collective-permute-start.34 = (f16[512,1024]{1,0:T(8,128)(2,1)S(1)}, f16[512,1024]{1,0:T(8,128)(2,1)}, u32[]{:S(2)}, u32[]{:S(2)}) collective-permute-start(f16[512,1024]{1,0:T(8,128)(2,1)S(1)} %convert_element_type.30), channel_id=1, source_target_pairs={{0,8},{2,10},{4,12},{6,14},{8,0},{10,2},{12,4},{14,6},{16,24},{18,... | collective-permute-start | bytes 3145736 | tf_op jit(solution)/shard_map/ppermute | solution.py:396
  12.6 23.4 %all-to-all-start = ((f32[4,256,128]{2,1,0:T(8,128)}), f32[4,256,128]{2,1,0:T(8,128)S(1)}, u32[]{:S(2)}, u32[]{:S(2)}) async-start(f32[4,256,128]{2,1,0:T(8,128)} %get-tuple-element.24), calls=%async_computation | async-start | bytes 1048576 | tf_op jit(solution)/shard_map/all_to_all | solution.py:393
  16.4 31.1 %collective-permute-start.12 = (bf16[128,1024]{1,0:T(8,128)(2,1)S(1)}, bf16[128,1024]{1,0:T(8,128)(2,1)S(1)}, u32[]{:S(2)}, u32[]{:S(2)}) collective-permute-start(bf16[128,1024]{1,0:T(8,128)(2,1)S(1)} %get-tuple-element.25), channel_id=1, source_target_pairs={{0,2},{2,0},{4,6},{6,4},{8,10},{10,8},{12,14},{14,12},{16,18},{18,... | collective-permute-start | bytes 786440 | tf_op jit(solution)/shard_map/ppermute | solution.py:396
  36.0 44.9 %all-to-all-start.2 = ((f16[4,128,1024]{2,1,0:T(8,128)(2,1)}), f16[4,128,1024]{2,1,0:T(8,128)(2,1)}, u32[]{:S(2)}, u32[]{:S(2)}) async-start(f16[4,128,1024]{2,1,0:T(8,128)(2,1)} %bitcast.1), calls=%async_computation.2 | async-start | bytes 2097152 | tf_op jit(solution)/shard_map/all_to_all | solution.py:393
  40.3 24.5 %collective-permute-start.13 = (bf16[128,1024]{1,0:T(8,128)(2,1)S(1)}, bf16[128,1024]{1,0:T(8,128)(2,1)S(1)}, u32[]{:S(2)}, u32[]{:S(2)}) collective-permute-start(bf16[128,1024]{1,0:T(8,128)(2,1)S(1)} %get-tuple-element.25), channel_id=1, source_target_pairs={{0,4},{2,6},{4,0},{6,2},{8,12},{10,14},{12,8},{14,10},{16,20},{18,... | collective-permute-start | bytes 786440 | tf_op jit(solution)/shard_map/ppermute | solution.py:396
  42.2 22.5 %collective-permute-start.14 = (bf16[128,1024]{1,0:T(8,128)(2,1)S(1)}, bf16[128,1024]{1,0:T(8,128)(2,1)S(1)}, u32[]{:S(2)}, u32[]{:S(2)}) collective-permute-start(bf16[128,1024]{1,0:T(8,128)(2,1)S(1)} %get-tuple-element.25), channel_id=1, source_target_pairs={{0,6},{2,4},{4,2},{6,0},{8,14},{10,12},{12,10},{14,8},{16,22},{18,... | collective-permute-start | bytes 786440 | tf_op jit(solution)/shard_map/ppermute | solution.py:396
  43.7 21.6 %collective-permute-start.23 = (bf16[128,1024]{1,0:T(8,128)(2,1)S(1)}, bf16[128,1024]{1,0:T(8,128)(2,1)S(1)}, u32[]{:S(2)}, u32[]{:S(2)}) collective-permute-start(bf16[128,1024]{1,0:T(8,128)(2,1)S(1)} %get-tuple-element.28), channel_id=1, source_target_pairs={{0,24},{2,26},{4,28},{6,30},{8,0},{10,2},{12,4},{14,6},{16,8},{18,... | collective-permute-start | bytes 786440 | tf_op jit(solution)/shard_map/ppermute | solution.py:396
  47.5 20.0 %collective-permute-start.15 = (bf16[128,1024]{1,0:T(8,128)(2,1)S(1)}, bf16[128,1024]{1,0:T(8,128)(2,1)S(1)}, u32[]{:S(2)}, u32[]{:S(2)}) collective-permute-start(bf16[128,1024]{1,0:T(8,128)(2,1)S(1)} %collective-permute-done.12.m1), channel_id=1, source_target_pairs={{0,1},{1,0},{2,3},{3,2},{4,5},{5,4},{6,7},{7,6},{8,9},{9,8},{10,11... | collective-permute-start | bytes 786440 | tf_op jit(solution)/shard_map/ppermute | solution.py:411
  64.8 4.1 %collective-permute-start.16 = (bf16[128,1024]{1,0:T(8,128)(2,1)S(1)}, bf16[128,1024]{1,0:T(8,128)(2,1)S(1)}, u32[]{:S(2)}, u32[]{:S(2)}) collective-permute-start(bf16[128,1024]{1,0:T(8,128)(2,1)S(1)} %collective-permute-done.13.m2), channel_id=1, source_target_pairs={{0,1},{1,0},{2,3},{3,2},{4,5},{5,4},{6,7},{7,6},{8,9},{9,8},{10,11... | collective-permute-start | bytes 786440 | tf_op jit(solution)/shard_map/ppermute | solution.py:411
  64.8 4.1 %collective-permute-start.17 = (bf16[128,1024]{1,0:T(8,128)(2,1)S(1)}, bf16[128,1024]{1,0:T(8,128)(2,1)S(1)}, u32[]{:S(2)}, u32[]{:S(2)}) collective-permute-start(bf16[128,1024]{1,0:T(8,128)(2,1)S(1)} %collective-permute-done.14.m3), channel_id=1, source_target_pairs={{0,1},{1,0},{2,3},{3,2},{4,5},{5,4},{6,7},{7,6},{8,9},{9,8},{10,11... | collective-permute-start | bytes 786440 | tf_op jit(solution)/shard_map/ppermute | solution.py:411
  65.3 9.2 %collective-permute-start.24 = (bf16[128,1024]{1,0:T(8,128)(2,1)S(1)}, bf16[128,1024]{1,0:T(8,128)(2,1)S(1)}, u32[]{:S(2)}, u32[]{:S(2)}) collective-permute-start(bf16[128,1024]{1,0:T(8,128)(2,1)S(1)} %broadcast_select_fusion.1.m0), channel_id=1, source_target_pairs={{0,2},{2,0},{4,6},{6,4},{8,10},{10,8},{12,14},{14,12},{16,18},{18,... | collective-permute-start | bytes 786440 | tf_op jit(solution)/shard_map/ppermute | solution.py:396
  66.9 13.6 %collective-permute-start.25 = (bf16[128,1024]{1,0:T(8,128)(2,1)S(1)}, bf16[128,1024]{1,0:T(8,128)(2,1)S(1)}, u32[]{:S(2)}, u32[]{:S(2)}) collective-permute-start(bf16[128,1024]{1,0:T(8,128)(2,1)S(1)} %broadcast_select_fusion.1.m0), channel_id=1, source_target_pairs={{0,4},{2,6},{4,0},{6,2},{8,12},{10,14},{12,8},{14,10},{16,20},{18,... | collective-permute-start | bytes 786440 | tf_op jit(solution)/shard_map/ppermute | solution.py:396
  67.4 13.0 %collective-permute-start.26 = (bf16[128,1024]{1,0:T(8,128)(2,1)S(1)}, bf16[128,1024]{1,0:T(8,128)(2,1)S(1)}, u32[]{:S(2)}, u32[]{:S(2)}) collective-permute-start(bf16[128,1024]{1,0:T(8,128)(2,1)S(1)} %broadcast_select_fusion.1.m0), channel_id=1, source_target_pairs={{0,6},{2,4},{4,2},{6,0},{8,14},{10,12},{12,10},{14,8},{16,22},{18,... | collective-permute-start | bytes 786440 | tf_op jit(solution)/shard_map/ppermute | solution.py:396
  72.7 10.6 %collective-permute-start.18 = (bf16[128,1024]{1,0:T(8,128)(2,1)S(1)}, bf16[128,1024]{1,0:T(8,128)(2,1)}, u32[]{:S(2)}, u32[]{:S(2)}) collective-permute-start(bf16[128,1024]{1,0:T(8,128)(2,1)S(1)} %get-tuple-element.26), channel_id=1, source_target_pairs={{0,8},{2,10},{4,12},{6,14},{8,16},{10,18},{12,20},{14,22},{16,24},... | collective-permute-start | bytes 786440 | tf_op jit(solution)/shard_map/ppermute | solution.py:396
  74.1 12.6 %collective-permute-start.27 = (bf16[128,1024]{1,0:T(8,128)(2,1)S(1)}, bf16[128,1024]{1,0:T(8,128)(2,1)S(1)}, u32[]{:S(2)}, u32[]{:S(2)}) collective-permute-start(bf16[128,1024]{1,0:T(8,128)(2,1)S(1)} %broadcast_select_fusion.1.m0), channel_id=1, source_target_pairs={{0,1},{1,0},{2,3},{3,2},{4,5},{5,4},{6,7},{7,6},{8,9},{9,8},{10,11... | collective-permute-start | bytes 786440 | tf_op jit(solution)/shard_map/ppermute | solution.py:411
  74.6 13.3 %collective-permute-start.28 = (bf16[128,1024]{1,0:T(8,128)(2,1)S(1)}, bf16[128,1024]{1,0:T(8,128)(2,1)S(1)}, u32[]{:S(2)}, u32[]{:S(2)}) collective-permute-start(bf16[128,1024]{1,0:T(8,128)(2,1)S(1)} %collective-permute-done.24.m1), channel_id=1, source_target_pairs={{0,1},{1,0},{2,3},{3,2},{4,5},{5,4},{6,7},{7,6},{8,9},{9,8},{10,11... | collective-permute-start | bytes 786440 | tf_op jit(solution)/shard_map/ppermute | solution.py:411
  80.4 8.2 %collective-permute-start.29 = (bf16[128,1024]{1,0:T(8,128)(2,1)S(1)}, bf16[128,1024]{1,0:T(8,128)(2,1)S(1)}, u32[]{:S(2)}, u32[]{:S(2)}) collective-permute-start(bf16[128,1024]{1,0:T(8,128)(2,1)S(1)} %collective-permute-done.25.m2), channel_id=1, source_target_pairs={{0,1},{1,0},{2,3},{3,2},{4,5},{5,4},{6,7},{7,6},{8,9},{9,8},{10,11... | collective-permute-start | bytes 786440 | tf_op jit(solution)/shard_map/ppermute | solution.py:411
  80.5 8.8 %collective-permute-start.30 = (bf16[128,1024]{1,0:T(8,128)(2,1)S(1)}, bf16[128,1024]{1,0:T(8,128)(2,1)}, u32[]{:S(2)}, u32[]{:S(2)}) collective-permute-start(bf16[128,1024]{1,0:T(8,128)(2,1)S(1)} %collective-permute-done.26.m3), channel_id=1, source_target_pairs={{0,1},{1,0},{2,3},{3,2},{4,5},{5,4},{6,7},{7,6},{8,9},{9,8},{10,11... | collective-permute-start | bytes 786440 | tf_op jit(solution)/shard_map/ppermute | solution.py:411
  83.3 23.6 %collective-permute-start.35 = (f16[128,1024]{1,0:T(8,128)(2,1)}, f16[128,1024]{1,0:T(8,128)(2,1)}, u32[]{:S(2)}, u32[]{:S(2)}) collective-permute-start(f16[128,1024]{1,0:T(8,128)(2,1)} %convert_element_type.34), channel_id=1, source_target_pairs={{0,16},{2,18},{4,20},{6,22},{8,24},{10,26},{12,28},{14,30},{16,0},... | collective-permute-start | bytes 786440 | tf_op jit(solution)/shard_map/ppermute | solution.py:396
  87.4 26.0 %collective-permute-start.19 = (bf16[128,1024]{1,0:T(8,128)(2,1)S(1)}, bf16[128,1024]{1,0:T(8,128)(2,1)}, u32[]{:S(2)}, u32[]{:S(2)}) collective-permute-start(bf16[128,1024]{1,0:T(8,128)(2,1)S(1)} %broadcast_select_fusion.2.xp), channel_id=1, source_target_pairs={{0,16},{2,18},{4,20},{6,22},{8,24},{10,26},{12,28},{14,30},{16,0},... | collective-permute-start | bytes 786440 | tf_op jit(solution)/shard_map/ppermute | solution.py:396
  102.8 20.8 %all-to-all-start.1 = ((bf16[4,128,256]{2,1,0:T(8,128)(2,1)}), bf16[4,128,256]{2,1,0:T(8,128)(2,1)}, u32[]{:S(2)}, u32[]{:S(2)}) async-start(bf16[4,128,256]{2,1,0:T(8,128)(2,1)} %copy-done.7), calls=%async_computation.1 | async-start | bytes 524288 | tf_op jit(solution)/shard_map/all_to_all | solution.py:393
  109.9 9.0 %collective-permute-start.36 = (bf16[128,1024]{1,0:T(8,128)(2,1)}, bf16[128,1024]{1,0:T(8,128)(2,1)S(1)}, u32[]{:S(2)}, u32[]{:S(2)}) collective-permute-start(bf16[128,1024]{1,0:T(8,128)(2,1)} %get-tuple-element.34), channel_id=1, source_target_pairs={{0,24},{2,26},{4,28},{6,30},{8,0},{10,2},{12,4},{14,6},{16,8},{18,... | collective-permute-start | bytes 786440 | tf_op jit(solution)/shard_map/ppermute | solution.py:396
  113.4 38.1 %collective-permute-start.20 = (bf16[128,1024]{1,0:T(8,128)(2,1)S(1)}, bf16[128,1024]{1,0:T(8,128)(2,1)S(1)}, u32[]{:S(2)}, u32[]{:S(2)}) collective-permute-start(bf16[128,1024]{1,0:T(8,128)(2,1)S(1)} %broadcast_select_fusion.3.x0.p0), channel_id=1, source_target_pairs={{0,2},{2,0},{4,6},{6,4},{8,10},{10,8},{12,14},{14,12},{16,18},{18,... | collective-permute-start | bytes 786440 | tf_op jit(solution)/shard_map/ppermute | solution.py:396
  123.6 56.2 %all-to-all-start.3 = ((f32[4,128,256]{2,1,0:T(8,128)}), f32[4,128,256]{2,1,0:T(8,128)S(1)}, u32[]{:S(2)}, u32[]{:S(2)}) async-start(f32[4,128,256]{2,1,0:T(8,128)} %fourth.1), calls=%async_computation.3 | async-start | bytes 1048576 | tf_op jit(solution)/shard_map/all_to_all | solution.py:393
  127.5 9.3 %collective-permute-start.10 = (bf16[128,1024]{1,0:T(8,128)(2,1)S(1)}, bf16[128,1024]{1,0:T(8,128)(2,1)S(1)}, u32[]{:S(2)}, u32[]{:S(2)}) collective-permute-start(bf16[128,1024]{1,0:T(8,128)(2,1)S(1)} %param.3), channel_id=1, source_target_pairs={{0,16},{2,18},{4,20},{6,22},{1,17},{3,19},{5,21},{7,23}} | collective-permute-start | bytes 786440 | tf_op jit(solution)/shard_map/cond/branch_3_fun/ppermute | solution.py:460
  130.8 11.4 %collective-permute-start.11 = (bf16[128,1024]{1,0:T(8,128)(2,1)S(1)}, bf16[128,1024]{1,0:T(8,128)(2,1)S(1)}, u32[]{:S(2)}, u32[]{:S(2)}) collective-permute-start(bf16[128,1024]{1,0:T(8,128)(2,1)S(1)} %param.3), channel_id=1, source_target_pairs={{0,24},{2,26},{4,28},{6,30},{1,25},{3,27},{5,29},{7,31}} | collective-permute-start | bytes 786440 | tf_op jit(solution)/shard_map/cond/branch_3_fun/ppermute | solution.py:460
  135.5 10.5 %collective-permute-start.9 = (bf16[128,1024]{1,0:T(8,128)(2,1)S(1)}, bf16[128,1024]{1,0:T(8,128)(2,1)S(1)}, u32[]{:S(2)}, u32[]{:S(2)}) collective-permute-start(bf16[128,1024]{1,0:T(8,128)(2,1)S(1)} %param.3), channel_id=1, source_target_pairs={{0,8},{2,10},{4,12},{6,14},{1,9},{3,11},{5,13},{7,15}} | collective-permute-start | bytes 786440 | tf_op jit(solution)/shard_map/cond/branch_3_fun/ppermute | solution.py:460
  146.1 20.4 %collective-permute-start.21 = (bf16[128,1024]{1,0:T(8,128)(2,1)S(1)}, bf16[128,1024]{1,0:T(8,128)(2,1)S(1)}, u32[]{:S(2)}, u32[]{:S(2)}) collective-permute-start(bf16[128,1024]{1,0:T(8,128)(2,1)S(1)} %broadcast_select_fusion.3.x0.p0), channel_id=1, source_target_pairs={{0,4},{2,6},{4,0},{6,2},{8,12},{10,14},{12,8},{14,10},{16,20},{18,... | collective-permute-start | bytes 786440 | tf_op jit(solution)/shard_map/ppermute | solution.py:396
  148.1 18.4 %collective-permute-start.22 = (bf16[128,1024]{1,0:T(8,128)(2,1)S(1)}, bf16[128,1024]{1,0:T(8,128)(2,1)S(1)}, u32[]{:S(2)}, u32[]{:S(2)}) collective-permute-start(bf16[128,1024]{1,0:T(8,128)(2,1)S(1)} %broadcast_select_fusion.3.x0.p0), channel_id=1, source_target_pairs={{0,6},{2,4},{4,2},{6,0},{8,14},{10,12},{12,10},{14,8},{16,22},{18,... | collective-permute-start | bytes 786440 | tf_op jit(solution)/shard_map/ppermute | solution.py:396
  149.5 23.9 %collective-permute-start.31 = (bf16[128,1024]{1,0:T(8,128)(2,1)S(1)}, bf16[128,1024]{1,0:T(8,128)(2,1)S(1)}, u32[]{:S(2)}, u32[]{:S(2)}) collective-permute-start(bf16[128,1024]{1,0:T(8,128)(2,1)S(1)} %get-tuple-element.37.x0), channel_id=1, source_target_pairs={{0,2},{2,0},{4,6},{6,4},{8,10},{10,8},{12,14},{14,12},{16,18},{18,... | collective-permute-start | bytes 786440 | tf_op jit(solution)/shard_map/ppermute | solution.py:396
  149.6 23.9 %collective-permute-start.32 = (bf16[128,1024]{1,0:T(8,128)(2,1)S(1)}, bf16[128,1024]{1,0:T(8,128)(2,1)S(1)}, u32[]{:S(2)}, u32[]{:S(2)}) collective-permute-start(bf16[128,1024]{1,0:T(8,128)(2,1)S(1)} %get-tuple-element.37.x0), channel_id=1, source_target_pairs={{0,4},{2,6},{4,0},{6,2},{8,12},{10,14},{12,8},{14,10},{16,20},{18,... | collective-permute-start | bytes 786440 | tf_op jit(solution)/shard_map/ppermute | solution.py:396
  151.6 21.9 %collective-permute-start.33 = (bf16[128,1024]{1,0:T(8,128)(2,1)S(1)}, bf16[128,1024]{1,0:T(8,128)(2,1)S(1)}, u32[]{:S(2)}, u32[]{:S(2)}) collective-permute-start(bf16[128,1024]{1,0:T(8,128)(2,1)S(1)} %get-tuple-element.37.x0), channel_id=1, source_target_pairs={{0,6},{2,4},{4,2},{6,0},{8,14},{10,12},{12,10},{14,8},{16,22},{18,... | collective-permute-start | bytes 786440 | tf_op jit(solution)/shard_map/ppermute | solution.py:396
  (22 other events, 92.7 us)
